TPU v7x, 32 devices: a whole 2x2x4 slice. The times are simulated.
32 devices in a mesh: tm: 8 (over z, x), space: 4 (over y, core).
Axes of the slice: x: 2, y: 2, z: 4, core: 2. Of those that a mesh axis runs over, the one named last changes fastest.
Arguments:
- snapshots: float32 [4224, 4096], P('tm', 'space')
- starts: int32 [32], replicated, may hold values from 0 to 3968, as said below
- freq_lines: int32 [128], replicated, may hold values from 0 to 128, as said below
Outputs:
- power_density: float32 [128, 4096], P(None, ('space', 'tm'))
- gram_matrices: float32 [2, 128, 32, 32], P(None, 'tm')
Inputs may be any that keep to these rules, and one draw needn't show every extreme that they name: starts never fall, and block b starts at most 64 snapshots away from b * 128; the first block starts at 0 and the last at 3968. `freq_lines`: distinct line numbers in any order; 0 and 128 are among them.
All inputs are finite; a program needn't handle non-finite values.
Results may differ from a plain program's by a relative error of at most 0.0001.
Values sent between devices are 32-bit elements; how exact they have to be, the bound alone decides.
No kernel may reach another device: no remote copies, remote signals or barrier semaphores. Data moves between devices by JAX's collectives and lax.ppermute only.
A program may use at most 64 MiB of HBM per device.

v0:
```python
import math
import jax
import jax.numpy as jnp
from jax import lax
from jax.sharding import PartitionSpec as P

NFFT = 256
NF = 128
NB = 32


def spectral_table(freq_lines):
    moments = jnp.arange(NFFT, dtype=jnp.int32)
    cycle = freq_lines[:, None] * moments[None, :] % NFFT
    angles = 2.0 * math.pi / NFFT * cycle.astype(jnp.float32)
    window = 0.5 - 0.5 * jnp.cos(2.0 * math.pi / NFFT * moments.astype(jnp.float32))
    window = window / jnp.sqrt(jnp.sum(window * window))
    return jnp.concatenate(
        [window[None, :] * jnp.cos(angles), -window[None, :] * jnp.sin(angles)], axis=0
    )


def block_spectra(series, starts, table):
    offsets = starts[:, None] + jnp.arange(NFFT, dtype=jnp.int32)[None, :]
    blocks = series[offsets]
    return jnp.einsum("kt,btp->kbp", table, blocks, precision=lax.Precision.HIGHEST)


def local_terms(spectra, factor):
    highest = lax.Precision.HIGHEST
    real_part = spectra[:NF]
    imag_part = spectra[NF:]
    power = jnp.sum(real_part * real_part + imag_part * imag_part, axis=1) / NB
    gram_real = jnp.einsum("fbp,fcp->fbc", real_part, real_part, precision=highest) + jnp.einsum(
        "fbp,fcp->fbc", imag_part, imag_part, precision=highest
    )
    gram_imag = jnp.einsum("fbp,fcp->fbc", real_part, imag_part, precision=highest) - jnp.einsum(
        "fbp,fcp->fbc", imag_part, real_part, precision=highest
    )
    return (power, jnp.stack([gram_real, gram_imag]) * factor)


def body(snapshots, starts, freq_lines):
    groups = lax.axis_size("tm")
    columns = snapshots.shape[1] // groups
    table = spectral_table(freq_lines)
    arranged = snapshots.reshape(snapshots.shape[0], groups, columns)
    spectra = block_spectra(
        lax.all_to_all(arranged, "tm", split_axis=1, concat_axis=0, tiled=True)[:, 0, :],
        starts,
        table,
    )
    total_points = columns * groups * lax.axis_size("space")
    power_density, own_gram = local_terms(spectra, 1.0 / (NB * total_points))
    per_device = NF // groups
    summed = lax.psum(own_gram, ("tm", "space"))
    gram_matrices = lax.dynamic_slice_in_dim(
        summed, lax.axis_index("tm") * per_device, per_device, 1
    )
    return (power_density, gram_matrices)


def solution(mesh):
    placed = (P("tm", "space"), P(), P())
    return jax.shard_map(
        body,
        mesh=mesh,
        in_specs=placed,
        out_specs=(P(None, ("space", "tm")), P(None, "tm", None, None)),
        check_vma=False,
    )
```

profile of v0, /device:TPU:0, one launch (start us, length us, event | category | flops | bytes accessed | tf_op | source)
XLA Modules:
  0.0 276.6 jit_solution(2760193698736418181)
XLA Ops:
  7.2 0.0 copy-start
  7.2 1.6 copy-done
  8.8 1.5 copy_bitcast_fusion
  10.3 0.0 copy-start.2
  10.3 0.0 copy-start.3
  10.3 7.4 %all-to-all-start = ((f32[528,8,128]{2,0,1:T(8,128)}), f32[528,8,128]{2,0,1:T(8,128)}, u32[]{:S(2)}, u32[]{:S(2)}) async-start(f32[528,8,128]{2,0,1:T(8,128)} %copy_bitcast_fusion), calls=%async_computation | async-start | bytes 4325376 | tf_op jit(solution)/shard_map/all_to_all | solution.py:49
  17.7 0.0 all-reduce.2.cloned.1.call-start
  17.7 0.6 multiply_reduce_fusion
  19.1 0.0 copy-done.2
  19.1 0.1 fusion.25
  19.2 0.0 copy-done.3
  19.2 0.6 cosine_multiply_fusion
  19.9 47.6 %all-to-all-done = f32[528,8,128]{2,0,1:T(8,128)} async-done(((f32[528,8,128]{2,0,1:T(8,128)}), f32[528,8,128]{2,0,1:T(8,128)}, u32[]{:S(2)}, u32[]{:S(2)}) %all-to-all-start) | async-done | bytes 2162720 | tf_op jit(solution)/shard_map/all_to_all | solution.py:49
  67.4 29.4 %gather_fusion = f32[8192,128]{1,0:T(8,128)} fusion(f32[4224,128]{1,0:T(8,128)} %bitcast.3, s32[8192]{0:T(1024)S(1)} %broadcast_clamp_fusion), kind=kCustom, calls=%fused_computation | custom fusion | bytes 8421376 | tf_op jit(solution)/shard_map/gather | solution.py:25
  96.8 5.6 %fusion.16 = f32[256,32,128]{2,0,1:T(8,128)S(1)} fusion(f32[32,256,128]{2,1,0:T(8,128)} %bitcast.23, f32[128,256]{1,0:T(8,128)S(1)} %get-tuple-element.8, f32[128,256]{1,0:T(8,128)S(1)} %get-tuple-element.7), kind=kOutput, calls=%fused_computation.17 | convolution fusion | flops 3221291008 | bytes 8650752 | tf_op jit(solution)/shard_map/kt,btp->kbp/dot_general | solution.py:26
  102.4 0.7 fusion.29
  103.1 0.0 copy-start.1
  103.1 5.7 %fusion.4 = f32[128,32,32]{2,1,0:T(8,128)} fusion(f32[128,32,128]{2,0,1:T(8,128)S(1)} %get-tuple-element.6), kind=kOutput, calls=%fused_computation.9 | convolution fusion | flops 201326592 | bytes 2621440 | tf_op jit(solution)/shard_map/fbp,fcp->fbc/dot_general | solution.py:34
  108.8 5.7 %fusion = f32[128,32,32]{2,1,0:T(8,128)S(1)} fusion(f32[128,32,128]{2,0,1:T(8,128)S(1)} %get-tuple-element.6, f32[128,32,128]{2,0,1:T(8,128)S(1)} %get-tuple-element.4), kind=kOutput, calls=%fused_computation.5 | convolution fusion | flops 201326592 | bytes 4718592 | tf_op jit(solution)/shard_map/fbp,fcp->fbc/dot_general | solution.py:37
  114.5 0.0 copy-done.1
  114.5 7.2 %subtract_bitcast_fusion = f32[1,128,32,32]{3,2,1,0:T(8,128)} fusion(f32[128,32,32]{2,1,0:T(8,128)S(1)} %fusion, f32[128,32,128]{2,0,1:T(8,128)S(1)} %get-tuple-element.6, f32[128,32,128]{2,0,1:T(8,128)S(1)} %get-tuple-element.4), kind=kOutput, calls=%fused_computation.2 | convolution fusion | flops 201457664 | bytes 5242880 | tf_op jit(solution)/shard_map/fbp,fcp->fbc/dot_general | solution.py:37
  121.7 2.7 copy.33
  124.3 9.7 %add_bitcast_fusion = f32[1,128,32,32]{3,2,1,0:T(8,128)} fusion(f32[128,32,32]{2,1,0:T(8,128)} %fusion.4, f32[128,32,128]{2,0,1:T(8,128)} %copy-done.1), kind=kOutput, calls=%fused_computation.3 | convolution fusion | flops 201457664 | bytes 3145728 | tf_op jit(solution)/shard_map/fbp,fcp->fbc/dot_general | solution.py:34
  134.1 2.7 copy.32
  136.7 1.1 maximum_multiply_fusion
  137.8 0.0 all-reduce.2.cloned.1.call-update
  137.9 0.6 broadcast_multiply_fusion
  138.5 128.4 %all-reduce.2.cloned.1.call-done = f32[2,128,32,32]{1,3,2,0:T(8,128)} async-done(((f32[2,128,32,32]{1,3,2,0:T(8,128)}), f32[2,128,32,32]{1,3,2,0:T(8,128)}) %all-reduce.2.cloned.1.call-update) | async-done | bytes 1048592 | tf_op jit(solution)/shard_map/psum | solution.py:56
  266.9 1.6 constant_dynamic-slice_fusion
  268.5 1.2 copy.34
  (3 shorter events, 0.1 us)
Async XLA Ops:
  7.2 1.6 copy-start
  10.3 8.8 %copy-start.2 = (s32[32]{0:T(128)S(1)}, s32[32]{0:T(128)}, u32[]{:S(2)}) copy-start(s32[32]{0:T(128)} %param.4) | copy-start | bytes 388
  10.3 9.0 %copy-start.3 = (s32[128]{0:T(128)S(1)}, s32[128]{0:T(128)}, u32[]{:S(2)}) copy-start(s32[128]{0:T(128)} %param.5) | copy-start | bytes 1540
  10.3 57.1 %all-to-all-start = ((f32[528,8,128]{2,0,1:T(8,128)}), f32[528,8,128]{2,0,1:T(8,128)}, u32[]{:S(2)}, u32[]{:S(2)}) async-start(f32[528,8,128]{2,0,1:T(8,128)} %copy_bitcast_fusion), calls=%async_computation | async-start | bytes 4325376 | tf_op jit(solution)/shard_map/all_to_all | solution.py:49
  17.7 249.3 %all-reduce.2.cloned.1.call-start = ((), (), s32[]{:S(2)}) async-start(), calls=%async_computation.1 | async-start | bytes 2097152 | tf_op jit(solution)/shard_map/psum | solution.py:56
  103.1 11.4 %copy-start.1 = (f32[128,32,128]{2,0,1:T(8,128)}, f32[128,32,128]{2,0,1:T(8,128)S(1)}, u32[]{:S(2)}) copy-start(f32[128,32,128]{2,0,1:T(8,128)S(1)} %get-tuple-element.4) | copy-start | bytes 6291460
Sparse Core Ops, SparseCore 0:
  138.0 128.9 all-reduce.1
where the time goes:
time: 277 us
  waiting for transfers between devices  176 us (64%)
  local copies, waits for them, and re-layouts  40.6 us (15%)
  matrix products  33.9 us (12%)
  between operations  14.8 us (5%)
  starting transfers between devices  7.42 us (3%)
  other arithmetic  3.87 us (1%)
    psum x1, waiting for transfers between devices, body(): summed = lax.psum(own_gram, ('tm', 'space'))  128 us
    all_to_all x1, waiting for transfers between devices, body(): lax.all_to_all(arranged, 'tm', split_axis=1, concat_axis=0, tiled=True)  47.6 us
    gather x1, local copies, waits for them, and re-layouts, block_spectra(): blocks = series[offsets]  29.4 us
    dot_general x1, matrix products, local_terms(): jnp.einsum('fbp,fcp->fbc', real_part, real_part, precision=highest)  9.72 us
    all_to_all x1, starting transfers between devices, body(): lax.all_to_all(arranged, 'tm', split_axis=1, concat_axis=0, tiled=True)  7.38 us
    dot_general x1, matrix products, local_terms(): jnp.einsum('fbp,fcp->fbc', real_part, imag_part, precision=highest)  7.21 us
    dot_general x1, matrix products, local_terms(): jnp.einsum('fbp,fcp->fbc', imag_part, imag_part, precision=highest)  5.68 us
    dot_general x1, matrix products, local_terms(): jnp.einsum('fbp,fcp->fbc', imag_part, real_part, precision=highest)  5.67 us
  transfers between devices with their start and end apart: 2, of which 2 were waited for; matrix products, arithmetic and copies ran while one was open for 1% of the time, Pallas kernels for 0%

commit v1 on v0

--- a/solution.py
+++ b/solution.py
@@ -7,6 +7,29 @@
 NFFT = 256
 NF = 128
 NB = 32
+
+
+def cut_along(x, dim, size):
+    lengths = x.shape
+    tiles = x.reshape(*lengths[:dim], size, lengths[dim] // size, *lengths[dim + 1 :])
+    return jnp.moveaxis(tiles, dim, 0)
+
+
+def joined_along(parts, dim):
+    shape = list(parts.shape[1:])
+    shape[dim] *= parts.shape[0]
+    return jnp.moveaxis(parts, 0, dim).reshape(shape)
+
+
+def sent_to_each(shard, axis, split_dim, concat_dim):
+    length, index = (lax.axis_size(axis), lax.axis_index(axis))
+    pieces = cut_along(shard, split_dim, length)
+    done = [pieces[index]]
+    for step in range(1, length):
+        sent = pieces[(index + step) % length]
+        done.append(lax.ppermute(sent, axis, [(i, (i + step) % length) for i in range(length)]))
+    pieces = jnp.stack(done)[(index - jnp.arange(length)) % length]
+    return joined_along(pieces, concat_dim)
 
 
 def spectral_table(freq_lines):
@@ -45,11 +68,7 @@
     columns = snapshots.shape[1] // groups
     table = spectral_table(freq_lines)
     arranged = snapshots.reshape(snapshots.shape[0], groups, columns)
-    spectra = block_spectra(
-        lax.all_to_all(arranged, "tm", split_axis=1, concat_axis=0, tiled=True)[:, 0, :],
-        starts,
-        table,
-    )
+    spectra = block_spectra(sent_to_each(arranged, "tm", 1, 0)[:, 0, :], starts, table)
     total_points = columns * groups * lax.axis_size("space")
     power_density, own_gram = local_terms(spectra, 1.0 / (NB * total_points))
     per_device = NF // groups

time: 277 us -> 280 us (1.011)
  starting transfers between devices: 7.42 us -> 17.4 us
  waiting for transfers between devices: 176 us -> 168 us
  local copies, waits for them, and re-layouts: 40.6 us -> 44.3 us
    all_to_all x1 -> x0, waiting for transfers between devices: 47.6 us -> none  [body(): lax.all_to_all(arranged, 'tm', split_axis=1, concat_axis=0, tiled=True)]
    ppermute x0 -> x7, waiting for transfers between devices: none -> 32.5 us  [sent_to_each(): lax.ppermute(sent, axis, [(i, (i + step) % length) for i in range(length)])]
    ppermute x0 -> x7, starting transfers between devices: none -> 17.4 us  [sent_to_each(): lax.ppermute(sent, axis, [(i, (i + step) % length) for i in range(length)])]
    all_to_all x1 -> x0, starting transfers between devices: 7.38 us -> none  [body(): lax.all_to_all(arranged, 'tm', split_axis=1, concat_axis=0, tiled=True)]
    psum x1, waiting for transfers between devices: 128 us -> 135 us  [body(): summed = lax.psum(own_gram, ('tm', 'space'))]
  transfers between devices with their start and end apart: 2 -> 8, of which waited for: 2 -> 3; matrix products, arithmetic and copies ran while one was open for 1% -> 1% of each run, Pallas kernels for 0% -> 0%
where the time goes in v1:
time: 280 us
  waiting for transfers between devices  168 us (60%)
  local copies, waits for them, and re-layouts  44.3 us (16%)
  matrix products  31.6 us (11%)
  starting transfers between devices  17.4 us (6%)
  between operations  15 us (5%)
  other arithmetic  3.9 us (1%)
    psum x1, waiting for transfers between devices, body(): summed = lax.psum(own_gram, ('tm', 'space'))  135 us
    ppermute x7, waiting for transfers between devices, sent_to_each(): lax.ppermute(sent, axis, [(i, (i + step) % length) for i in range(length)])  32.5 us
    gather x1, local copies, waits for them, and re-layouts, block_spectra(): blocks = series[offsets]  27.9 us
    ppermute x7, starting transfers between devices, sent_to_each(): lax.ppermute(sent, axis, [(i, (i + step) % length) for i in range(length)])  17.4 us
    dot_general x1, matrix products, local_terms(): jnp.einsum('fbp,fcp->fbc', real_part, real_part, precision=highest)  7.39 us
    dot_general x1, matrix products, local_terms(): jnp.einsum('fbp,fcp->fbc', real_part, imag_part, precision=highest)  7.21 us
    dot_general x1, matrix products, local_terms(): jnp.einsum('fbp,fcp->fbc', imag_part, imag_part, precision=highest)  5.72 us
    dot_general x1, matrix products, local_terms(): jnp.einsum('fbp,fcp->fbc', imag_part, real_part, precision=highest)  5.67 us
  transfers between devices with their start and end apart: 8, of which 3 were waited for; matrix products, arithmetic and copies ran while one was open for 1% of the time, Pallas kernels for 0%

profile of v1, /device:TPU:0, one launch (start us, length us, event | category | flops | bytes accessed | tf_op | source)
XLA Modules:
  0.0 279.7 jit_solution(622454791731893518)
XLA Ops:
  7.2 0.0 all-reduce.2.cloned.1.call-start
  7.3 2.1 copy.32
  9.4 0.0 copy-start.1
  9.5 0.0 copy-start.2
  9.5 2.4 constant_dynamic-slice_fusion.1
  11.9 5.0 %collective-permute-start.5 = (f32[528,1,128]{2,0,1:T(8,128)S(1)}, f32[528,1,128]{2,0,1:T(8,128)S(1)}, u32[]{:S(2)}, u32[]{:S(2)}) collective-permute-start(f32[528,1,128]{2,0,1:T(8,128)S(1)} %bitcast.50), channel_id=1, source_target_pairs={{0,24},{4,28},{8,0},{12,4},{16,8},{20,12},{24,16},{28,20},{1,25},{... | collective-permute-start | bytes 811016 | tf_op jit(solution)/shard_map/ppermute | solution.py:30
  16.9 1.4 collective-permute-start.6
  18.3 0.0 collective-permute-start.4
  18.3 1.6 collective-permute-start.1
  19.9 1.9 collective-permute-start
  21.8 0.6 multiply_reduce_fusion
  23.2 0.0 copy-done.1
  23.2 0.1 fusion.25
  23.3 0.0 copy-done.2
  23.3 0.6 cosine_multiply_fusion
  24.0 17.9 %collective-permute-done = f32[528,1,128]{2,0,1:T(8,128)S(1)} collective-permute-done((f32[528,1,128]{2,0,1:T(8,128)}, f32[528,1,128]{2,0,1:T(8,128)S(1)}, u32[]{:S(2)}, u32[]{:S(2)}) %collective-permute-start) | collective-permute-done | bytes 270368 | tf_op jit(solution)/shard_map/ppermute | solution.py:30
  41.9 0.7 collective-permute-start.2
  42.5 0.0 collective-permute-done.1
  42.5 6.8 %collective-permute-start.3 = (f32[528,1,128]{2,0,1:T(8,128)}, f32[528,1,128]{2,0,1:T(8,128)S(1)}, u32[]{:S(2)}, u32[]{:S(2)}) collective-permute-start(f32[528,1,128]{2,0,1:T(8,128)} %bitcast.52), channel_id=1, source_target_pairs={{0,16},{4,20},{8,24},{12,28},{16,0},{20,4},{24,8},{28,12},{1,17},{... | collective-permute-start | bytes 811016 | tf_op jit(solution)/shard_map/ppermute | solution.py:30
  49.4 14.6 %collective-permute-done.2 = f32[528,1,128]{2,0,1:T(8,128)S(1)} collective-permute-done((f32[528,1,128]{2,0,1:T(8,128)}, f32[528,1,128]{2,0,1:T(8,128)S(1)}, u32[]{:S(2)}, u32[]{:S(2)}) %collective-permute-start.2) | collective-permute-done | bytes 270368 | tf_op jit(solution)/shard_map/ppermute | solution.py:30
  64.0 0.0 collective-permute-done.3
  64.1 0.0 collective-permute-done.4
  64.1 0.0 collective-permute-done.5
  64.2 0.0 collective-permute-done.6
  64.2 0.0 copy-start
  64.2 1.3 copy-done
  65.5 2.3 gather_fusion
  67.8 27.9 %gather_fusion.1 = f32[8192,128]{1,0:T(8,128)} fusion(f32[4224,128]{1,0:T(8,128)S(1)} %bitcast.43, s32[8192]{0:T(1024)S(1)} %broadcast_clamp_fusion), kind=kCustom, calls=%fused_computation.1 | custom fusion | bytes 8421376 | tf_op jit(solution)/shard_map/gather | solution.py:48
  95.7 5.6 %fusion.16 = f32[256,32,128]{2,0,1:T(8,128)S(1)} fusion(f32[32,256,128]{2,1,0:T(8,128)} %bitcast.44, f32[128,256]{1,0:T(8,128)S(1)} %get-tuple-element.16, f32[128,256]{1,0:T(8,128)S(1)} %get-tuple-element.15), kind=kOutput, calls=%fused_computation.24 | convolution fusion | flops 3221291008 | bytes 8650752 | tf_op jit(solution)/shard_map/kt,btp->kbp/dot_general | solution.py:49
  101.3 0.7 fusion.31
  102.1 5.7 %fusion.4 = f32[128,32,32]{2,1,0:T(8,128)} fusion(f32[128,32,128]{2,0,1:T(8,128)S(1)} %get-tuple-element.6), kind=kOutput, calls=%fused_computation.9 | convolution fusion | flops 201326592 | bytes 2621440 | tf_op jit(solution)/shard_map/fbp,fcp->fbc/dot_general | solution.py:57
  107.8 5.7 %fusion = f32[128,32,32]{2,1,0:T(8,128)S(1)} fusion(f32[128,32,128]{2,0,1:T(8,128)S(1)} %get-tuple-element.6, f32[128,32,128]{2,0,1:T(8,128)S(1)} %get-tuple-element.4), kind=kOutput, calls=%fused_computation.5 | convolution fusion | flops 201326592 | bytes 4718592 | tf_op jit(solution)/shard_map/fbp,fcp->fbc/dot_general | solution.py:60
  113.5 7.2 %subtract_bitcast_fusion = f32[1,128,32,32]{3,2,1,0:T(8,128)} fusion(f32[128,32,32]{2,1,0:T(8,128)S(1)} %fusion, f32[128,32,128]{2,0,1:T(8,128)S(1)} %get-tuple-element.6, f32[128,32,128]{2,0,1:T(8,128)S(1)} %get-tuple-element.4), kind=kOutput, calls=%fused_computation.2 | convolution fusion | flops 201457664 | bytes 5242880 | tf_op jit(solution)/shard_map/fbp,fcp->fbc/dot_general | solution.py:60
  120.7 2.7 copy.30
  123.3 7.4 %add_bitcast_fusion = f32[1,128,32,32]{3,2,1,0:T(8,128)} fusion(f32[128,32,32]{2,1,0:T(8,128)} %fusion.4, f32[128,32,128]{2,0,1:T(8,128)S(1)} %get-tuple-element.4), kind=kOutput, calls=%fused_computation.3 | convolution fusion | flops 201457664 | bytes 3145728 | tf_op jit(solution)/shard_map/fbp,fcp->fbc/dot_general | solution.py:57
  130.7 2.7 copy.29
  133.4 1.1 maximum_multiply_fusion
  134.5 0.0 all-reduce.2.cloned.1.call-update
  134.5 0.6 broadcast_multiply_fusion
  135.2 135.0 %all-reduce.2.cloned.1.call-done = f32[2,128,32,32]{1,3,2,0:T(8,128)} async-done(((f32[2,128,32,32]{1,3,2,0:T(8,128)}), f32[2,128,32,32]{1,3,2,0:T(8,128)}) %all-reduce.2.cloned.1.call-update) | async-done | bytes 1048592 | tf_op jit(solution)/shard_map/psum | solution.py:75
  270.1 1.6 constant_dynamic-slice_fusion
  271.7 1.2 copy.31
  (13 shorter events, 0.3 us)
Async XLA Ops:
  7.2 263.0 %all-reduce.2.cloned.1.call-start = ((), (), s32[]{:S(2)}) async-start(), calls=%async_computation | async-start | bytes 2097152 | tf_op jit(solution)/shard_map/psum | solution.py:75
  9.4 13.7 %copy-start.1 = (s32[32]{0:T(128)S(1)}, s32[32]{0:T(128)}, u32[]{:S(2)}) copy-start(s32[32]{0:T(128)} %param.4) | copy-start | bytes 388
  9.5 13.8 %copy-start.2 = (s32[128]{0:T(128)S(1)}, s32[128]{0:T(128)}, u32[]{:S(2)}) copy-start(s32[128]{0:T(128)} %param.5) | copy-start | bytes 1540
  11.9 52.3 %collective-permute-start.5 = (f32[528,1,128]{2,0,1:T(8,128)S(1)}, f32[528,1,128]{2,0,1:T(8,128)S(1)}, u32[]{:S(2)}, u32[]{:S(2)}) collective-permute-start(f32[528,1,128]{2,0,1:T(8,128)S(1)} %bitcast.50), channel_id=1, source_target_pairs={{0,24},{4,28},{8,0},{12,4},{16,8},{20,12},{24,16},{28,20},{1,25},{... | collective-permute-start | bytes 811016 | tf_op jit(solution)/shard_map/ppermute | solution.py:30
  16.9 47.3 %collective-permute-start.6 = (f32[528,1,128]{2,0,1:T(8,128)S(1)}, f32[528,1,128]{2,0,1:T(8,128)S(1)}, u32[]{:S(2)}, u32[]{:S(2)}) collective-permute-start(f32[528,1,128]{2,0,1:T(8,128)S(1)} %bitcast.49), channel_id=1, source_target_pairs={{0,28},{4,0},{8,4},{12,8},{16,12},{20,16},{24,20},{28,24},{1,29},{... | collective-permute-start | bytes 811016 | tf_op jit(solution)/shard_map/ppermute | solution.py:30
  18.3 45.8 %collective-permute-start.4 = (f32[528,1,128]{2,0,1:T(8,128)S(1)}, f32[528,1,128]{2,0,1:T(8,128)S(1)}, u32[]{:S(2)}, u32[]{:S(2)}) collective-permute-start(f32[528,1,128]{2,0,1:T(8,128)S(1)} %bitcast.51), channel_id=1, source_target_pairs={{0,20},{4,24},{8,28},{12,0},{16,4},{20,8},{24,12},{28,16},{1,21},{... | collective-permute-start | bytes 811016 | tf_op jit(solution)/shard_map/ppermute | solution.py:30
  18.3 24.3 %collective-permute-start.1 = (f32[528,1,128]{2,0,1:T(8,128)}, f32[528,1,128]{2,0,1:T(8,128)S(1)}, u32[]{:S(2)}, u32[]{:S(2)}) collective-permute-start(f32[528,1,128]{2,0,1:T(8,128)} %bitcast.4), channel_id=1, source_target_pairs={{0,8},{4,12},{8,16},{12,20},{16,24},{20,28},{24,0},{28,4},{1,9},{5... | collective-permute-start | bytes 811016 | tf_op jit(solution)/shard_map/ppermute | solution.py:30
  19.9 22.0 %collective-permute-start = (f32[528,1,128]{2,0,1:T(8,128)}, f32[528,1,128]{2,0,1:T(8,128)S(1)}, u32[]{:S(2)}, u32[]{:S(2)}) collective-permute-start(f32[528,1,128]{2,0,1:T(8,128)} %bitcast.2), channel_id=1, source_target_pairs={{0,4},{4,8},{8,12},{12,16},{16,20},{20,24},{24,28},{28,0},{1,5},{5... | collective-permute-start | bytes 811016 | tf_op jit(solution)/shard_map/ppermute | solution.py:30
  41.9 22.2 %collective-permute-start.2 = (f32[528,1,128]{2,0,1:T(8,128)}, f32[528,1,128]{2,0,1:T(8,128)S(1)}, u32[]{:S(2)}, u32[]{:S(2)}) collective-permute-start(f32[528,1,128]{2,0,1:T(8,128)} %bitcast.53), channel_id=1, source_target_pairs={{0,12},{4,16},{8,20},{12,24},{16,28},{20,0},{24,4},{28,8},{1,13},{... | collective-permute-start | bytes 811016 | tf_op jit(solution)/shard_map/ppermute | solution.py:30
  42.5 21.5 %collective-permute-start.3 = (f32[528,1,128]{2,0,1:T(8,128)}, f32[528,1,128]{2,0,1:T(8,128)S(1)}, u32[]{:S(2)}, u32[]{:S(2)}) collective-permute-start(f32[528,1,128]{2,0,1:T(8,128)} %bitcast.52), channel_id=1, source_target_pairs={{0,16},{4,20},{8,24},{12,28},{16,0},{20,4},{24,8},{28,12},{1,17},{... | collective-permute-start | bytes 811016 | tf_op jit(solution)/shard_map/ppermute | solution.py:30
  64.2 1.4 copy-start
Sparse Core Ops, SparseCore 0:
  134.6 135.4 all-reduce.1
